TPU v7x, 32 devices: a whole 2x2x4 slice. The times are simulated.
32 devices in a mesh: row: 4 (over y, x), col: 8 (over z, core).
Axes of the slice: x: 2, y: 2, z: 4, core: 2. Of those that a mesh axis runs over, the one named last changes fastest.
Arguments:
- amps_old: bfloat16 [1024, 262144], P(('row', 'col')), may hold values from -6 to 6
- other_terms: bfloat16 [1024, 262144], P(('row', 'col')), may hold values from -6 to 6
- occ_energy: float32 [32], replicated, may hold values from -1.5 to -0.5
- virt_energy: float32 [512], replicated, may hold values from 0.2 to 1.5
- integrals: bfloat16 [1024, 262144], P('row', 'col'), may hold values from -0.1875 to 0.1875
Outputs:
- amps_new: bfloat16 [1024, 262144], P(('row', 'col'))
All inputs are finite; a program needn't handle non-finite values.
Results may differ from a plain program's by a relative error of at most 0.0055.
Values may be sent and summed in bfloat16 or wider, within the bound.
No kernel may reach another device: no remote copies, remote signals or barrier semaphores. Data moves between devices by JAX's collectives and lax.ppermute only.
A program may use at most 320 MiB of HBM per device.

v0:
```python
import jax
import jax.numpy as jnp
from jax import lax
from jax.sharding import PartitionSpec as P


def pair_energy(pairs, occ_energy):
    count = occ_energy.shape[0]
    first = pairs // count
    second = pairs % count
    grid = jnp.arange(count, dtype=jnp.int32)
    e_first = jnp.sum(jnp.where(first[:, None] == grid[None, :], occ_energy[None, :], 0.0), axis=1)
    e_second = jnp.sum(
        jnp.where(second[:, None] == grid[None, :], occ_energy[None, :], 0.0), axis=1
    )
    return e_first + e_second


def local(amps_old, other_terms, occ_energy, virt_energy, integrals):
    n_row = lax.axis_size("row")
    n_col = lax.axis_size("col")
    row_id = lax.axis_index("row")
    col_id = lax.axis_index("col")
    per_dev = amps_old.shape[0]
    cd_dev = integrals.shape[0]
    window = amps_old[:, : cd_dev * n_row]
    row_pairs = lax.all_gather(window, "col", axis=0, tiled=True)
    panel = lax.all_to_all(row_pairs, "row", split_axis=1, concat_axis=0, tiled=True)
    ladder = lax.psum_scatter(
        jnp.dot(panel, integrals, preferred_element_type=jnp.float32).astype(jnp.bfloat16),
        "row",
        scatter_dimension=0,
        tiled=True,
    ).astype(jnp.float32)
    virt_all = (virt_energy[:, None] + virt_energy[None, :]).reshape(-1)
    first_pair = (row_id * n_col + col_id) * per_dev
    own_pairs = first_pair + jnp.arange(per_dev, dtype=jnp.int32)
    denom_pairs = pair_energy(own_pairs, occ_energy)[:, None] - virt_all[None, :]
    moved = lax.all_to_all(
        ladder.astype(jnp.bfloat16), "col", split_axis=0, concat_axis=1, tiled=True
    ).astype(ladder.dtype)
    increment = (moved / denom_pairs).astype(jnp.bfloat16)
    updated = (
        amps_old.astype(jnp.float32)
        + other_terms.astype(jnp.float32) / denom_pairs
        + increment.astype(jnp.float32)
    )
    return updated.astype(jnp.bfloat16)


def solution(mesh):
    return jax.shard_map(
        local,
        mesh=mesh,
        in_specs=(P(("row", "col"), None), P(("row", "col"), None), P(), P(), P("row", "col")),
        out_specs=P(("row", "col"), None),
        check_vma=False,
    )
```

profile of v0, /device:TPU:0, one launch (start us, length us, event | category | flops | bytes accessed | tf_op | source)
XLA Modules:
  0.0 1049.0 jit_solution(17985617899202413814)
XLA Ops:
  6.5 0.0 reduce-scatter.4.cloned.1.call-start
  6.5 0.8 slice.3
  7.4 16.5 %all_gather.3 = bf16[256,1024]{1,0:T(8,128)(2,1)S(1)} all-gather(bf16[32,1024]{1,0:T(8,128)(2,1)S(1)} %slice.3), channel_id=1, replica_groups=mesh['row'=4,'col'=8] {'col'}, dimensions={0}, use_global_device_ids=true | all-gather | bytes 589824 | tf_op jit(solution)/shard_map/all_gather | solution.py:27
  23.9 0.2 copy.14
  24.1 12.5 %all_to_all.32 = bf16[256,4,256]{0,2,1:T(8,128)(2,1)S(1)} all-to-all(bf16[256,4,256]{0,2,1:T(8,128)(2,1)S(1)} %bitcast.18), channel_id=1, replica_groups=mesh['row'=4,'col'=8] {'row'}, dimensions={1} | all-to-all | bytes 1048576 | tf_op jit(solution)/shard_map/all_to_all | solution.py:28
  36.6 0.2 copy.15
  36.8 30.6 %convolution_convert_fusion = bf16[1024,32768]{1,0:T(8,128)(2,1)} fusion(bf16[1024,256]{1,0:T(8,128)(2,1)S(1)} %bitcast.16, bf16[256,32768]{1,0:T(8,128)(2,1)} %param.9), kind=kOutput, calls=%fused_computation | convolution fusion | flops 17213423616 | bytes 84410368 | tf_op jit(solution)/shard_map/dot_general | solution.py:30
  67.4 0.0 reduce-scatter.4.cloned.1.call-update
  67.4 0.0 copy-start
  67.4 0.0 copy-start.1
  67.5 557.9 %reduce-scatter.4.cloned.1.call-done = bf16[256,32768]{1,0:T(8,128)(2,1)} async-done(((bf16[1024,32768]{1,0:T(8,128)(2,1)}), bf16[256,32768]{1,0:T(8,128)(2,1)}) %reduce-scatter.4.cloned.1.call-update) | async-done | bytes 16777232
  625.4 5.8 all-to-all-start.1
  631.1 0.0 copy-done
  631.1 0.1 add_bitcast_fusion
  631.3 0.3 copy.18
  631.6 0.0 copy-done.1
  631.6 0.2 select_reduce_fusion
  631.8 363.0 %all-to-all-done.1 = bf16[8,32,32768]{2,1,0:T(8,128)(2,1)} async-done(((bf16[8,32,32768]{2,1,0:T(8,128)(2,1)}), bf16[8,32,32768]{2,1,0:T(8,128)(2,1)}, u32[]{:S(2)}, u32[]{:S(2)}) %all-to-all-start.1) | async-done | bytes 16777248 | tf_op jit(solution)/shard_map/all_to_all | solution.py:39
  994.8 8.5 convert_bitcast_fusion
  1003.3 11.2 %copy.17 = f32[8,4,8,32768]{3,2,0,1:T(8,128)} copy(f32[8,4,8,32768]{3,2,1,0:T(8,128)S(1)} %convert_bitcast_fusion) | data formatting | bytes 67108864 | tf_op jit(solution)/shard_map/convert_element_type | solution.py:41
  1014.5 27.6 %fusion.3 = bf16[32,262144]{1,0:T(8,128)(2,1)} fusion(bf16[32,262144]{1,0:T(8,128)(2,1)} %param.6, bf16[32,262144]{1,0:T(8,128)(2,1)} %param.5, f32[32,262144]{1,0:T(8,128)} %bitcast.14, f32[262144]{0:T(1024)S(1)} %bitcast.17, f32[32]{0:T(128)S(1)} %add.70), kind=kLoop, calls=%fused_computation.7 | loop fusion | flops 83886080 | bytes 84934784 | tf_op jit(solution)/shard_map/convert_element_type | solution.py:48
  (2 shorter events, 0.0 us)
Async XLA Ops:
  6.5 618.8 %reduce-scatter.4.cloned.1.call-start = ((), (), s32[]{:S(2)}) async-start(), calls=%async_computation.3 | async-start | bytes 83886080
  67.4 563.7 %copy-start = (f32[512]{0:T(512)S(1)}, f32[512]{0:T(512)}, u32[]{:S(2)}) copy-start(f32[512]{0:T(512)} %param.8) | copy-start | bytes 6148
  67.4 564.1 %copy-start.1 = (f32[32]{0:T(128)S(1)}, f32[32]{0:T(128)}, u32[]{:S(2)}) copy-start(f32[32]{0:T(128)} %param.7) | copy-start | bytes 388
  625.4 369.4 %all-to-all-start.1 = ((bf16[8,32,32768]{2,1,0:T(8,128)(2,1)}), bf16[8,32,32768]{2,1,0:T(8,128)(2,1)}, u32[]{:S(2)}, u32[]{:S(2)}) async-start(bf16[8,32,32768]{2,1,0:T(8,128)(2,1)} %bitcast.15), calls=%async_computation.1 | async-start | bytes 33554432 | tf_op jit(solution)/shard_map/all_to_all | solution.py:39
Sparse Core Ops, SparseCore 0:
  67.6 557.7 reduce-scatter.3
where the time goes:
time: 1050 us
  waiting for transfers between devices  921 us (88%)
  other arithmetic  36.5 us (3%)
  matrix products  30.6 us (3%)
  blocking collectives  29 us (3%)
  between operations  13.5 us (1%)
  local copies, waits for them, and re-layouts  12.7 us (1%)
    unnamed x2, waiting for transfers between devices  558 us
    all_to_all x1, waiting for transfers between devices, local(): lax.all_to_all(ladder.astype(jnp.bfloat16), 'col', split_axis=0, concat_a...  363 us
    dot_general x1, matrix products, local(): jnp.dot(panel, integrals, preferred_element_type=jnp.float32)  30.6 us
    convert_element_type x1, other arithmetic, local(): return updated.astype(jnp.bfloat16)  27.6 us
  transfers between devices with their start and end apart: 2, of which 2 were waited for; matrix products, arithmetic and copies ran while one was open for 0% of the time, Pallas kernels for 0%

commit v1 on v0

--- a/solution.py
+++ b/solution.py
@@ -1,7 +1,20 @@
+import functools
 import jax
 import jax.numpy as jnp
 from jax import lax
 from jax.sharding import PartitionSpec as P
+
+
+def _review_types(content, mesh_dim):
+    return jnp.concatenate(
+        lax.all_to_all(
+            jnp.stack(jnp.split(content, lax.axis_size(mesh_dim), axis=0)), mesh_dim, 0, 0
+        ),
+        axis=1,
+    )
+
+
+set_thing = functools.partial(_review_types, mesh_dim="col")
 
 
 def pair_energy(pairs, occ_energy):
@@ -36,9 +49,7 @@
     first_pair = (row_id * n_col + col_id) * per_dev
     own_pairs = first_pair + jnp.arange(per_dev, dtype=jnp.int32)
     denom_pairs = pair_energy(own_pairs, occ_energy)[:, None] - virt_all[None, :]
-    moved = lax.all_to_all(
-        ladder.astype(jnp.bfloat16), "col", split_axis=0, concat_axis=1, tiled=True
-    ).astype(ladder.dtype)
+    moved = set_thing(ladder.astype(jnp.bfloat16)).astype(ladder.dtype)
     increment = (moved / denom_pairs).astype(jnp.bfloat16)
     updated = (
         amps_old.astype(jnp.float32)

time: 1050 us -> 1640 us (1.56)
  waiting for transfers between devices: 921 us -> 1480 us
  local copies, waits for them, and re-layouts: 12.7 us -> 42 us
    unnamed x2, waiting for transfers between devices: 558 us -> 1110 us
    unnamed x5 -> x15, local copies, waits for them, and re-layouts: 0.28 us -> 25.9 us
where the time goes in v1:
time: 1640 us
  waiting for transfers between devices  1480 us (90%)
  local copies, waits for them, and re-layouts  42 us (3%)
  other arithmetic  36.5 us (2%)
  matrix products  30.7 us (2%)
  blocking collectives  29 us (2%)
    unnamed x2, waiting for transfers between devices  1110 us
    all_to_all x1, waiting for transfers between devices, _review_types(): lax.all_to_all(jnp.stack(jnp.split(content, lax.axis_size(mesh_dim), axis...  363 us
  transfers between devices with their start and end apart: 2, of which 2 were waited for; matrix products, arithmetic and copies ran while one was open for 0% of the time, Pallas kernels for 0%

profile of v1, /device:TPU:0, one launch (start us, length us, event | category | flops | bytes accessed | tf_op | source)
XLA Modules:
  0.0 1635.9 jit_solution(11836754688429700646)
XLA Ops:
  6.5 0.0 all-reduce.3.cloned.1.call-start
  6.5 0.8 slice.3
  7.4 16.5 %all_gather.3 = bf16[256,1024]{1,0:T(8,128)(2,1)S(1)} all-gather(bf16[32,1024]{1,0:T(8,128)(2,1)S(1)} %slice.3), channel_id=1, replica_groups=mesh['row'=4,'col'=8] {'col'}, dimensions={0}, use_global_device_ids=true | all-gather | bytes 589824 | tf_op jit(solution)/shard_map/all_gather | solution.py:40
  23.9 0.2 copy.13
  24.1 12.5 all_to_all.24
  36.6 0.2 copy.14
  36.8 30.7 %convolution_convert_fusion = bf16[1024,32768]{1,0:T(8,128)(2,1)} fusion(bf16[1024,256]{1,0:T(8,128)(2,1)S(1)} %bitcast.46, bf16[256,32768]{1,0:T(8,128)(2,1)} %param.9), kind=kOutput, calls=%fused_computation | convolution fusion | flops 17213423616 | bytes 84410368 | tf_op jit(solution)/shard_map/dot_general | solution.py:43
  67.5 0.0 copy-start.2
  67.5 0.0 all-reduce.3.cloned.1.call-update
  67.6 0.6 copy-done.2
  68.2 0.6 dynamic-slice
  69.4 1114.7 %all-reduce.3.cloned.1.call-done = bf16[1024,32768]{1,0:T(8,128)(2,1)} async-done(((bf16[1024,32768]{1,0:T(8,128)(2,1)}), bf16[1024,32768]{1,0:T(8,128)(2,1)}) %all-reduce.3.cloned.1.call-update) | async-done | bytes 67108880
  1184.1 3.0 fusion.11
  1187.1 3.6 fusion.10
  1190.7 3.6 fusion.9
  1194.3 3.6 fusion.8
  1197.8 3.6 fusion.7
  1201.4 3.6 fusion.6
  1205.0 3.6 fusion.5
  1208.5 3.6 fusion.4
  1212.1 0.0 copy-start
  1212.1 0.0 copy-start.1
  1212.1 5.9 all-to-all-start.1
  1218.0 0.0 copy-done
  1218.0 0.1 add_bitcast_fusion
  1218.1 0.3 copy.17
  1218.5 0.0 copy-done.1
  1218.5 0.2 select_reduce_fusion
  1218.7 363.0 %all-to-all-done.1 = bf16[8,32,32768]{2,1,0:T(8,128)(2,1)} async-done(((bf16[8,32,32768]{2,1,0:T(8,128)(2,1)}), bf16[8,32,32768]{2,1,0:T(8,128)(2,1)}, u32[]{:S(2)}, u32[]{:S(2)}) %all-to-all-start.1) | async-done | bytes 16777248 | tf_op jit(solution)/shard_map/all_to_all | solution.py:10
  1581.6 8.5 convert_bitcast_fusion
  1590.2 11.2 copy.16
  1601.4 27.6 %fusion.3 = bf16[32,262144]{1,0:T(8,128)(2,1)} fusion(bf16[32,262144]{1,0:T(8,128)(2,1)} %param.6, bf16[32,262144]{1,0:T(8,128)(2,1)} %param.5, f32[32,262144]{1,0:T(8,128)} %bitcast.45, f32[262144]{0:T(1024)S(1)} %bitcast.47, f32[32]{0:T(128)S(1)} %add.70), kind=kLoop, calls=%fused_computation.7 | loop fusion | flops 83886080 | bytes 84934784 | tf_op jit(solution)/shard_map/convert_element_type | solution.py:59
  (2 shorter events, 0.0 us)
Async XLA Ops:
  6.5 1177.6 %all-reduce.3.cloned.1.call-start = ((), (), s32[]{:S(2)}) async-start(), calls=%async_computation.2 | async-start | bytes 134217728
  67.5 0.7 copy-start.2
  1212.1 5.9 copy-start
  1212.1 6.4 copy-start.1
  1212.1 369.5 %all-to-all-start.1 = ((bf16[8,32,32768]{2,1,0:T(8,128)(2,1)}), bf16[8,32,32768]{2,1,0:T(8,128)(2,1)}, u32[]{:S(2)}, u32[]{:S(2)}) async-start(bf16[8,32,32768]{2,1,0:T(8,128)(2,1)} %fusion.4), calls=%async_computation.1 | async-start | bytes 33554432 | tf_op jit(solution)/shard_map/all_to_all | solution.py:10
Sparse Core Ops, SparseCore 0:
  67.7 1116.3 all-reduce.2
